TPU v7x, 256 devices: a whole 4x4x8 slice. The times are simulated.
256 devices in a mesh: dp: 16 (over z, core), tm: 16 (over x, y).
Axes of the slice: x: 4, y: 4, z: 8, core: 2. Of those that a mesh axis runs over, the one named last changes fastest.
Arguments:
- video_tokens: bfloat16 [16, 128, 196, 768], P('dp', 'tm'), may hold values from -6 to 6
- norm_gain: bfloat16 [768], P('dp'), may hold values from 0.25 to 1.75
- norm_bias: bfloat16 [768], P('dp'), may hold values from -3 to 3
- qkv_weight: bfloat16 [768, 1152], P('dp'), may hold values from -16 to 16
- frame_counts: int32 [16], P('dp'), may hold values from 16 to 128, as said below
- clip_starts: int32 [16, 8], P('dp'), may hold values 0 or 1
- frame_kept: int32 [16, 128], P('dp'), may hold values 0 or 1
- attended_grad: bfloat16 [16, 128, 196, 384], P('dp', 'tm'), may hold values from -6 to 6
Outputs:
- attended: bfloat16 [16, 128, 196, 384], P('dp', 'tm')
- tokens_grad: bfloat16 [16, 128, 196, 768], P('dp', 'tm')
- qkv_weight_grad: float32 [768, 1152], P('dp')
- gain_grad: float32 [768], P('dp')
- bias_grad: float32 [768], P('dp')
Inputs may be any that keep to these rules, and one draw needn't show every extreme that they name: `frame_counts`: every count is a multiple of 16; some video has 128 frames and some video has 16.
All inputs are finite; a program needn't handle non-finite values. No bound on the sum of `clip_starts` or of `frame_kept` on one device may be relied on, other than what follows from the above.
Results may differ from a plain program's by a relative error of at most 0.02.
Values may be sent and summed in bfloat16 or wider, within the bound.
A program may use at most 128 MiB of HBM per device.

v0:
```python
import jax
import jax.numpy as jnp
from jax import lax
from jax.sharding import PartitionSpec as P

HEADS = 6
BLOCK = 16


masked_value = -1e30
epsilon = 1e-05


def standardize(rows):
    centred = rows - jnp.mean(rows, axis=-1, keepdims=True)
    inverse = lax.rsqrt(jnp.mean(centred * centred, axis=-1, keepdims=True) + epsilon)
    return (centred * inverse, inverse)


def frame_masks(frame_count, starts, kept, frames):
    frame_index = jnp.arange(frames, dtype=jnp.int32)
    block_index = jnp.arange(starts.shape[0], dtype=jnp.int32)
    flags = jnp.where(block_index > 0, starts, 0)
    clip_of_block = jnp.cumsum(flags)
    member = (frame_index // BLOCK)[:, None] == block_index[None, :]
    clip_number = jnp.sum(jnp.where(member, clip_of_block[None, :], 0), axis=1)
    usable = (frame_index < frame_count) & (kept == 1)
    same_clip = clip_number[:, None] == clip_number[None, :]
    allowed = same_clip & (usable[None, :] | (frame_index[:, None] == frame_index[None, :]))
    return (allowed, frame_index < frame_count)


def split_heads(projected, start, joined):
    return projected[:, :, start : start + joined].reshape(
        projected.shape[0], projected.shape[1], HEADS, joined // HEADS
    )


def attend(projected, allowed, valid):
    frames, patch_rows = (projected.shape[0], projected.shape[1])
    joined = projected.shape[2] // 3
    scale = (joined // HEADS) ** (-0.5)
    queries = split_heads(projected, 0, joined)
    key_rows = split_heads(projected, joined, joined)
    values = split_heads(projected, 2 * joined, joined)
    scores = (
        jnp.einsum("fphd,gphd->phfg", queries, key_rows, preferred_element_type=jnp.float32) * scale
    )
    scores = jnp.where(allowed, scores, masked_value)
    shifted = jnp.exp(scores - jnp.max(scores, axis=-1, keepdims=True))
    weights = shifted / jnp.sum(shifted, axis=-1, keepdims=True)
    mixed = jnp.einsum(
        "phfg,gphd->fphd", weights.astype(jnp.bfloat16), values, preferred_element_type=jnp.float32
    )
    mixed = jnp.where(valid[:, None, None, None], mixed, 0.0)
    return (mixed.reshape(frames, patch_rows, joined).astype(jnp.bfloat16), weights)


def attend_back(projected, weights, upstream, valid):
    frames, patch_rows = (projected.shape[0], projected.shape[1])
    joined = projected.shape[2] // 3
    head_width = joined // HEADS
    scale = head_width ** (-0.5)
    queries = split_heads(projected, 0, joined)
    key_rows = split_heads(projected, joined, joined)
    values = split_heads(projected, 2 * joined, joined)
    kept_grad = jnp.where(valid[:, None, None], upstream, jnp.zeros_like(upstream))
    kept_grad = kept_grad.reshape(frames, patch_rows, HEADS, head_width)
    rounded = weights.astype(jnp.bfloat16)
    weight_grad = jnp.einsum(
        "fphd,gphd->phfg", kept_grad, values, preferred_element_type=jnp.float32
    )
    value_grad = jnp.einsum(
        "phfg,fphd->gphd", rounded, kept_grad, preferred_element_type=jnp.float32
    )
    inner = jnp.sum(weight_grad * weights, axis=-1, keepdims=True)
    score_grad = (weights * (weight_grad - inner) * scale).astype(jnp.bfloat16)
    query_grad = jnp.einsum(
        "phfg,gphd->fphd", score_grad, key_rows, preferred_element_type=jnp.float32
    )
    key_grad = jnp.einsum(
        "phfg,fphd->gphd", score_grad, queries, preferred_element_type=jnp.float32
    )
    parts = [query_grad, key_grad, value_grad]
    return jnp.concatenate(
        [piece.reshape(frames, patch_rows, joined) for piece in parts], axis=2
    ).astype(jnp.bfloat16)


def to_patches(block_rows, tm_count):
    patches = block_rows.shape[1]
    padded = -(-patches // tm_count) * tm_count
    widened = jnp.pad(block_rows, ((0, 0), (0, padded - patches), (0, 0)))
    return lax.all_to_all(widened, "tm", split_axis=1, concat_axis=0, tiled=True)


def to_frames(patch_rows, patches):
    regrouped = lax.all_to_all(patch_rows, "tm", split_axis=0, concat_axis=1, tiled=True)
    return regrouped[:, :patches]


def body(
    video_tokens,
    norm_gain,
    norm_bias,
    qkv_weight,
    frame_counts,
    clip_starts,
    frame_kept,
    attended_grad,
):
    tm_count = lax.axis_size("tm")
    weight_full, gain_full, bias_full = (
        lax.all_gather(qkv_weight, "dp", axis=0, tiled=True),
        lax.all_gather(norm_gain, "dp", axis=0, tiled=True),
        lax.all_gather(norm_bias, "dp", axis=0, tiled=True),
    )
    frames_dev, patches, model_width = (
        video_tokens.shape[1],
        video_tokens.shape[2],
        video_tokens.shape[3],
    )
    columns = weight_full.shape[1]
    frames_all = frames_dev * tm_count
    gain_wide = gain_full.astype(jnp.float32)
    standard, inverse = standardize(video_tokens.reshape(-1, model_width).astype(jnp.float32))
    normed = (standard * gain_wide + bias_full.astype(jnp.float32)).astype(jnp.bfloat16)
    allowed, valid = frame_masks(frame_counts[0], clip_starts[0], frame_kept[0], frames_all)
    upstream = attended_grad[0]
    contract_rows = (((0,), (0,)), ((), ()))
    contract_cols = (((1,), (1,)), ((), ()))
    projected = jnp.dot(normed, weight_full, preferred_element_type=jnp.float32).astype(
        jnp.bfloat16
    )
    projected_patch = to_patches(projected.reshape(frames_dev, patches, columns), tm_count)
    mixed, weights = attend(projected_patch, allowed, valid)
    attended = to_frames(mixed, patches)
    grad_patch = to_patches(upstream, tm_count)
    projected_grad = to_frames(
        attend_back(projected_patch, weights, grad_patch, valid), patches
    ).reshape(-1, columns)
    weight_grad = lax.dot_general(
        normed, projected_grad, contract_rows, preferred_element_type=jnp.float32
    )
    normed_grad = lax.dot_general(
        projected_grad, weight_full, contract_cols, preferred_element_type=jnp.float32
    )
    normed_grad = lax.optimization_barrier(normed_grad.astype(jnp.bfloat16)).astype(jnp.float32)
    gain_part = jnp.sum(normed_grad * standard, axis=0)
    bias_part = jnp.sum(normed_grad, axis=0)
    scaled = normed_grad * gain_wide
    tokens_grad = inverse * (
        scaled
        - jnp.mean(scaled, axis=-1, keepdims=True)
        - standard * jnp.mean(scaled * standard, axis=-1, keepdims=True)
    )
    tokens_grad = tokens_grad.astype(jnp.bfloat16).reshape(1, frames_dev, patches, model_width)
    shares = (
        lax.psum_scatter(
            weight_grad.astype(jnp.bfloat16), "dp", scatter_dimension=0, tiled=True
        ).astype(jnp.float32),
        lax.psum_scatter(
            gain_part.astype(jnp.bfloat16), "dp", scatter_dimension=0, tiled=True
        ).astype(jnp.float32),
        lax.psum_scatter(
            bias_part.astype(jnp.bfloat16), "dp", scatter_dimension=0, tiled=True
        ).astype(jnp.float32),
    )
    weight_total, gain_total, bias_total = (
        lax.psum(shares[0].astype(jnp.bfloat16), "tm").astype(jnp.float32),
        lax.psum(shares[1].astype(jnp.bfloat16), "tm").astype(jnp.float32),
        lax.psum(shares[2].astype(jnp.bfloat16), "tm").astype(jnp.float32),
    )
    attended = attended.reshape(1, frames_dev, patches, attended.shape[2])
    return (attended, tokens_grad, weight_total, gain_total, bias_total)


def solution(mesh):
    placed = (
        P("dp", "tm", None, None),
        P("dp"),
        P("dp"),
        P("dp", None),
        P("dp"),
        P("dp", None),
        P("dp", None),
        P("dp", "tm", None, None),
    )
    return jax.shard_map(
        body,
        mesh=mesh,
        in_specs=placed,
        out_specs=(
            P("dp", "tm", None, None),
            P("dp", "tm", None, None),
            P("dp", None),
            P("dp"),
            P("dp"),
        ),
        check_vma=False,
    )
```

profile of v0, /device:TPU:24, one launch (start us, length us, event | category | flops | bytes accessed | tf_op | source)
XLA Modules:
  0.0 463.8 jit_solution(9911502411266005399)
XLA Ops:
  7.9 2.4 pad.9
  10.4 7.2 %all-to-all-start.2 = ((bf16[8,208,384]{2,0,1:T(8,128)(2,1)}), bf16[8,208,384]{2,0,1:T(8,128)(2,1)}, u32[]{:S(2)}, u32[]{:S(2)}) async-start(bf16[8,208,384]{2,0,1:T(8,128)(2,1)} %pad.9), calls=%async_computation.2 | async-start | bytes 2555904 | tf_op jit(solution)/shard_map/all_to_all | solution.py:94
  19.0 2.7 copy.121
  23.4 29.5 %all-reduce.8 = (bf16[768]{0:T(1024)(128)(2,1)S(1)}, bf16[768]{0:T(1024)(128)(2,1)S(1)}) all-reduce(bf16[768]{0:T(1024)(128)(2,1)S(1)} %dynamic-update-slice.1, bf16[768]{0:T(1024)(128)(2,1)S(1)} %dynamic-update-slice), channel_id=1, replica_groups=mesh['dp'=16,'tm'=16] {'dp'}, use_global_device_ids=true, to_apply=%add.3 | all-reduce | flops 1536 | bytes 6144
  53.1 5.2 %reshape.199 = f32[1568,768]{1,0:T(8,128)} reshape(f32[1,8,196,768]{3,2,1,0:T(8,128)} %copy.121) | data formatting | bytes 9633792 | tf_op jit(solution)/shard_map/convert_element_type | solution.py:126
  58.3 8.4 %convolution_convert_fusion = bf16[1568,1152]{1,0:T(8,128)(2,1)} fusion(bf16[768,1152]{1,0:T(8,128)(2,1)} %all-gather.2.cloned.1.call-done, f32[1568,768]{1,0:T(8,128)} %reshape.199, f32[768]{0:T(1024)S(1)} %convert_element_type.84, f32[768]{0:T(1024)S(1)} %convert_element_type.83, f32[1568]{0:T(1024)S(1)} %rsqrt.13, f32[1568]{0:T(1024)S(1)} %div.31), kind=kOutput, calls=%fused_computation.2 | convolution fusion | flops 2782359552 | bytes 10217728 | tf_op jit(solution)/shard_map/dot_general | solution.py:132
  66.7 4.7 %reshape.187 = bf16[8,196,1152]{2,1,0:T(8,128)(2,1)} reshape(bf16[1568,1152]{1,0:T(8,128)(2,1)} %convolution_convert_fusion) | data formatting | bytes 7225344 | tf_op jit(solution)/shard_map/reshape | solution.py:135
  71.3 2.5 copy.155
  73.8 2.2 pad.8.clone
  76.0 7.0 %all-to-all-start = ((bf16[8,208,1152]{2,0,1:T(8,128)(2,1)}), bf16[8,208,1152]{2,0,1:T(8,128)(2,1)}, u32[]{:S(2)}, u32[]{:S(2)}) async-start(bf16[8,208,1152]{2,0,1:T(8,128)(2,1)} %pad.8.clone), calls=%async_computation | async-start | bytes 7667712 | tf_op jit(solution)/shard_map/all_to_all | solution.py:94
  84.1 2.5 copy.159
  86.7 5.1 %all_to_all.63 = bf16[128,13,6,64]{3,2,0,1:T(8,128)(2,1)} reshape(bf16[16,8,13,384]{3,1,0,2:T(8,128)(2,1)} %bitcast.68) | data formatting | bytes 2555904 | tf_op jit(solution)/shard_map/all_to_all | solution.py:94
  91.7 4.1 broadcast_select_fusion
  95.9 4.5 copy.135
  100.4 28.8 %all-to-all-done = bf16[8,208,1152]{2,0,1:T(8,128)(2,1)} async-done(((bf16[8,208,1152]{2,0,1:T(8,128)(2,1)}), bf16[8,208,1152]{2,0,1:T(8,128)(2,1)}, u32[]{:S(2)}, u32[]{:S(2)}) %all-to-all-start) | async-done | bytes 3833888 | tf_op jit(solution)/shard_map/all_to_all | solution.py:94
  129.2 2.6 copy.158
  131.8 2.1 fusion.48
  133.9 2.5 copy.129
  136.3 2.5 copy.128
  138.8 2.5 copy.127
  141.3 4.9 %fusion.51 = f32[13,6,128,128]{2,3,1,0:T(8,128)} fusion(bf16[128,13,6,64]{0,3,2,1:T(8,128)(2,1)} %copy.135, bf16[128,13,6,64]{0,3,2,1:T(8,128)(2,1)} %bitcast.69), kind=kOutput, calls=%fused_computation.76 | convolution fusion | flops 163577856 | bytes 7667712 | tf_op jit(solution)/shard_map/fphd,gphd->phfg/dot_general | solution.py:70
  146.2 5.8 %fusion.50 = (f32[13,6,128]{2,1,0:T(8,128)S(1)}, f32[13,6,128,128]{2,3,1,0:T(8,128)}) fusion(pred[128,128]{0,1:T(8,128)(4,1)S(1)} %fusion.40, bf16[128,13,6,64]{0,3,2,1:T(8,128)(2,1)} %bitcast.74, bf16[128,13,6,64]{0,3,2,1:T(8,128)(2,1)} %bitcast.72), kind=kOutput, calls=%fused_computation.75 | convolution fusion | flops 168689792 | bytes 7724032 | tf_op jit(solution)/shard_map/sub | solution.py:50
  152.0 10.0 %fusion.29 = bf16[13,6,64,128]{3,2,1,0:T(8,128)(2,1)} fusion(bf16[128,13,6,64]{0,3,2,1:T(8,128)(2,1)} %bitcast.73, f32[13,6,128,128]{2,3,1,0:T(8,128)} %fusion.51, f32[13,6,128,128]{2,3,1,0:T(8,128)} %get-tuple-element.50, f32[13,6,128]{2,1,0:T(8,128)S(1)} %get-tuple-element.49), kind=kOutput, calls=%fused_computation.42 | convolution fusion | flops 173172608 | bytes 12819456 | tf_op jit(solution)/shard_map/phfg,gphd->fphd/dot_general | solution.py:78
  162.0 10.1 %fusion.32 = bf16[13,6,64,128]{3,2,1,0:T(8,128)(2,1)} fusion(bf16[128,13,6,64]{0,3,2,1:T(8,128)(2,1)} %bitcast.75, f32[13,6,128,128]{2,3,1,0:T(8,128)} %fusion.51, f32[13,6,128,128]{2,3,1,0:T(8,128)} %get-tuple-element.50, f32[13,6,128]{2,1,0:T(8,128)S(1)} %get-tuple-element.49), kind=kOutput, calls=%fused_computation.43 | convolution fusion | flops 173172608 | bytes 12819456 | tf_op jit(solution)/shard_map/phfg,fphd->gphd/dot_general | solution.py:81
  172.1 5.8 %convolution_convert_fusion.3 = bf16[13,6,64,128]{3,2,1,0:T(8,128)(2,1)} fusion(bf16[128,13,6,64]{0,3,2,1:T(8,128)(2,1)} %copy.135, f32[13,6,128,128]{2,3,1,0:T(8,128)} %get-tuple-element.50, f32[13,6,128]{2,1,0:T(8,128)S(1)} %get-tuple-element.49), kind=kOutput, calls=%fused_computation.44 | convolution fusion | flops 166772736 | bytes 7707648 | tf_op jit(solution)/shard_map/phfg,fphd->gphd/dot_general | solution.py:73
  177.9 3.0 copy.140
  180.9 3.0 copy.141
  183.9 2.9 copy.142
  186.8 4.1 pad_maximum_fusion
  190.8 7.3 %all-to-all-start.3 = ((bf16[128,13,1152]{2,1,0:T(8,128)(2,1)}), bf16[128,13,1152]{2,1,0:T(8,128)(2,1)}, u32[]{:S(2)}, u32[]{:S(2)}) async-start(bf16[128,13,1152]{2,1,0:T(8,128)(2,1)} %pad_maximum_fusion), calls=%async_computation.3 | async-start | bytes 9437184 | tf_op jit(solution)/shard_map/all_to_all | solution.py:98
  200.1 2.1 convert_element_type.96
  202.2 53.1 %all-to-all-done.3 = bf16[128,13,1152]{2,1,0:T(8,128)(2,1)} async-done(((bf16[128,13,1152]{2,1,0:T(8,128)(2,1)}), bf16[128,13,1152]{2,1,0:T(8,128)(2,1)}, u32[]{:S(2)}, u32[]{:S(2)}) %all-to-all-start.3) | async-done | bytes 3833888 | tf_op jit(solution)/shard_map/all_to_all | solution.py:98
  255.3 3.2 copy.144
  258.8 2.3 copy.145
  261.1 4.7 %reshape.197 = bf16[1568,1152]{1,0:T(8,128)(2,1)} reshape(bf16[8,196,1152]{2,1,0:T(8,128)(2,1)} %copy.145) | data formatting | bytes 7225344 | tf_op jit(solution)/shard_map/reshape | solution.py:141
  265.8 7.9 %convolution_convert_fusion.1 = bf16[768,1152]{1,0:T(8,128)(2,1)} fusion(bf16[1568,768]{1,0:T(8,128)(2,1)} %convert_element_type.96, bf16[1568,1152]{1,0:T(8,128)(2,1)} %reshape.197), kind=kOutput, calls=%fused_computation.27 | convolution fusion | flops 2775416832 | bytes 7790592 | tf_op jit(solution)/shard_map/dot_general | solution.py:142
  273.6 3.3 select_convert_fusion
  276.9 2.3 copy.131
  279.2 5.5 %all-to-all-start.1 = ((bf16[128,13,384]{2,1,0:T(8,128)(2,1)}), bf16[128,13,384]{2,1,0:T(8,128)(2,1)S(1)}, u32[]{:S(2)}, u32[]{:S(2)}) async-start(bf16[128,13,384]{2,1,0:T(8,128)(2,1)} %copy.131), calls=%async_computation.1 | async-start | bytes 3145728 | tf_op jit(solution)/shard_map/all_to_all | solution.py:98
  285.6 16.6 %all-to-all-done.1 = bf16[128,13,384]{2,1,0:T(8,128)(2,1)S(1)} async-done(((bf16[128,13,384]{2,1,0:T(8,128)(2,1)}), bf16[128,13,384]{2,1,0:T(8,128)(2,1)S(1)}, u32[]{:S(2)}, u32[]{:S(2)}) %all-to-all-start.1) | async-done | bytes 1277984 | tf_op jit(solution)/shard_map/all_to_all | solution.py:98
  304.6 5.0 %convolution_convert_fusion.2 = bf16[1568,768]{1,0:T(8,128)(2,1)S(1)} fusion(bf16[1568,1152]{1,0:T(8,128)(2,1)S(1)} %copy-done.2, bf16[768,1152]{1,0:T(8,128)(2,1)} %all-gather.2.cloned.1.call-done), kind=kOutput, calls=%fused_computation.28 | convolution fusion | flops 2775736320 | bytes 7790592 | tf_op jit(solution)/shard_map/dot_general | solution.py:145
  310.1 4.4 fusion.10
  314.5 53.4 %all-reduce.7 = (bf16[768]{0:T(1024)(128)(2,1)S(1)}, bf16[768]{0:T(1024)(128)(2,1)S(1)}) all-reduce(bf16[768]{0:T(1024)(128)(2,1)S(1)} %get-tuple-element.35, bf16[768]{0:T(1024)(128)(2,1)S(1)} %reduce_sum.92), channel_id=3, replica_groups=mesh['dp'=16,'tm'=16] {'dp'}, use_global_device_ids=true, to_apply=%region_12.13.clone | all-reduce | flops 1536 | bytes 6144
  368.1 4.3 fusion.8
  372.4 34.8 %all-reduce.6 = (bf16[48]{0:T(256)(128)(2,1)S(1)}, bf16[48]{0:T(256)(128)(2,1)S(1)}) all-reduce(bf16[48]{0:T(256)(128)(2,1)S(1)} %dynamic-slice.3, bf16[48]{0:T(256)(128)(2,1)S(1)} %dynamic-slice.5), channel_id=1, replica_groups=mesh['dp'=16,'tm'=16] {'tm'}, use_global_device_ids=true, to_apply=%region_13.14 | all-reduce | flops 96 | bytes 384 | tf_op jit(solution)/shard_map/psum | solution.py:171
  408.2 2.6 reshape.198
  410.8 1.9 copy.148
  412.7 43.1 %all-reduce.11.cloned.1.call-done = bf16[48,1152]{1,0:T(8,128)(2,1)} async-done(((bf16[48,1152]{1,0:T(8,128)(2,1)}), bf16[48,1152]{1,0:T(8,128)(2,1)}) %all-reduce.11.cloned.1.call-update) | async-done | bytes 110608 | tf_op jit(solution)/shard_map/psum | solution.py:170
  (61 shorter events, 12.0 us)
Async XLA Ops:
  7.2 10.4 %copy-start = (bf16[1,8,196,768]{3,1,2,0:T(8,128)(2,1)S(1)}, bf16[1,8,196,768]{3,1,2,0:T(8,128)(2,1)}, u32[]{:S(2)}) copy-start(bf16[1,8,196,768]{3,1,2,0:T(8,128)(2,1)} %param.8) | copy-start | bytes 7225348
  7.2 51.1 %all-gather.2.cloned.1.call-start = ((), (), s32[]{:S(2)}) async-start(), calls=%async_computation.5 | async-start | bytes 1880064 | tf_op jit(solution)/shard_map/all_gather | solution.py:114
  10.4 65.7 %all-to-all-start.2 = ((bf16[8,208,384]{2,0,1:T(8,128)(2,1)}), bf16[8,208,384]{2,0,1:T(8,128)(2,1)}, u32[]{:S(2)}, u32[]{:S(2)}) async-start(bf16[8,208,384]{2,0,1:T(8,128)(2,1)} %pad.9), calls=%async_computation.2 | async-start | bytes 2555904 | tf_op jit(solution)/shard_map/all_to_all | solution.py:94
  18.9 2.8 copy-start.3
  18.9 4.0 copy-start.4
  18.9 4.3 copy-start.5
  76.0 7.7 %copy-start.6 = (s32[1,8]{1,0:T(1,128)S(1)}, s32[1,8]{1,0:T(1,128)}, u32[]{:S(2)}) copy-start(s32[1,8]{1,0:T(1,128)} %param.13) | copy-start | bytes 100
  76.0 8.0 %copy-start.7 = (s32[1,128]{1,0:T(1,128)S(1)}, s32[1,128]{1,0:T(1,128)}, u32[]{:S(2)}) copy-start(s32[1,128]{1,0:T(1,128)} %param.14) | copy-start | bytes 1540
  76.0 53.2 %all-to-all-start = ((bf16[8,208,1152]{2,0,1:T(8,128)(2,1)}), bf16[8,208,1152]{2,0,1:T(8,128)(2,1)}, u32[]{:S(2)}, u32[]{:S(2)}) async-start(bf16[8,208,1152]{2,0,1:T(8,128)(2,1)} %pad.8.clone), calls=%async_computation | async-start | bytes 7667712 | tf_op jit(solution)/shard_map/all_to_all | solution.py:94
  190.8 64.4 %all-to-all-start.3 = ((bf16[128,13,1152]{2,1,0:T(8,128)(2,1)}), bf16[128,13,1152]{2,1,0:T(8,128)(2,1)}, u32[]{:S(2)}, u32[]{:S(2)}) async-start(bf16[128,13,1152]{2,1,0:T(8,128)(2,1)} %pad_maximum_fusion), calls=%async_computation.3 | async-start | bytes 9437184 | tf_op jit(solution)/shard_map/all_to_all | solution.py:98
  198.1 169.9 %reduce-scatter.2.cloned.1.call-start = ((), (), s32[]{:S(2)}) async-start(), calls=%async_computation.6 | async-start | bytes 1880064 | tf_op jit(solution)/shard_map/reduce_scatter | solution.py:159
  265.8 7.9 %copy-start.1 = (bf16[128,13,384]{0,2,1:T(8,128)(2,1)S(1)}, bf16[128,13,384]{0,2,1:T(8,128)(2,1)}, u32[]{:S(2)}) copy-start(bf16[128,13,384]{0,2,1:T(8,128)(2,1)} %copy.127) | copy-start | bytes 3833860
  279.2 23.0 %all-to-all-start.1 = ((bf16[128,13,384]{2,1,0:T(8,128)(2,1)}), bf16[128,13,384]{2,1,0:T(8,128)(2,1)S(1)}, u32[]{:S(2)}, u32[]{:S(2)}) async-start(bf16[128,13,384]{2,1,0:T(8,128)(2,1)} %copy.131), calls=%async_computation.1 | async-start | bytes 3145728 | tf_op jit(solution)/shard_map/all_to_all | solution.py:98
  284.7 171.1 %all-reduce.11.cloned.1.call-start = ((), (), s32[]{:S(2)}) async-start(), calls=%async_computation.7 | async-start | bytes 221184 | tf_op jit(solution)/shard_map/psum | solution.py:170
  302.2 2.5 copy-start.2
Sparse Core Ops, SparseCore 0:
  9.8 41.8 all-gather.1
  273.8 84.6 reduce-scatter.1
  368.2 87.4 all-reduce.10
where the time goes:
time: 467 us; the launch traced here: 464 us
  waiting for transfers between devices  142 us (30%)
  blocking collectives  118 us (25%)
  local copies, waits for them, and re-layouts  76.8 us (16%)
  matrix products  61.1 us (13%)
  starting transfers between devices  27.5 us (6%)
  other arithmetic  22.6 us (5%)
  between operations  15.9 us (3%)
    unnamed x2, blocking collectives  82.9 us
    all_to_all x2, waiting for transfers between devices, to_frames(): lax.all_to_all(patch_rows, 'tm', split_axis=0, concat_axis=1, tiled=True)  69.6 us
    psum x1, waiting for transfers between devices, body(): lax.psum(shares[0].astype(jnp.bfloat16), 'tm').astype(jnp.float32)  43.1 us
    psum x1, blocking collectives, body(): lax.psum(shares[1].astype(jnp.bfloat16), 'tm').astype(jnp.float32)  34.8 us
    all_to_all x2, waiting for transfers between devices, to_patches(): lax.all_to_all(widened, 'tm', split_axis=1, concat_axis=0, tiled=True)  28.8 us
    all_to_all x2, starting transfers between devices, to_patches(): lax.all_to_all(widened, 'tm', split_axis=1, concat_axis=0, tiled=True)  14.2 us
    all_to_all x2, starting transfers between devices, to_frames(): lax.all_to_all(patch_rows, 'tm', split_axis=0, concat_axis=1, tiled=True)  12.7 us
    all_to_all x3, local copies, waits for them, and re-layouts, to_patches(): lax.all_to_all(widened, 'tm', split_axis=1, concat_axis=0, tiled=True)  10.2 us
  transfers between devices with their start and end apart: 7, of which 4 were waited for; matrix products, arithmetic and copies ran while one was open for 16% of the time, Pallas kernels for 0%

commit v1 on v0

v1 whole, which is shorter than its diff:
```python
import functools

import jax
import jax.numpy as jnp
from jax import lax
from jax.experimental import pallas as pl
from jax.experimental.pallas import tpu as pltpu
from jax.sharding import PartitionSpec as P

F32 = jnp.float32
BF = jnp.bfloat16
MESH = pl.DeviceIdType.MESH
BLOCK = 16
FR = 128
D = 768
C = 1152
HD = 384
EPS = 1e-05
MASKED = -1e30
OFFS = [(dx, dy) for dx in range(4) for dy in range(4) if (dx, dy) != (0, 0)]
WB = 56
NN = (((1,), (0,)), ((), ()))
NT = (((1,), (1,)), ((), ()))
TN = (((0,), (0,)), ((), ()))


def dot(a, b, dims=NN):
    return lax.dot_general(a, b, dims, preferred_element_type=F32)


def wait(ref, sem):
    pltpu.make_async_copy(ref, ref, sem).wait()


def kernel(
    xt, gt, wl, mask, valid,
    ato, tgo, dwo, gbo,
    xbuf, gbuf, abuf, tbuf, wall, wfull, wt, dw, gb,
    normed, mst, rst, proj, dproj, nt, ng, gacc, bacc,
    senda, recva, sendb, recvb, totb, crx, red, fin,
    pk, pkp, pk2, pkz, pk3, pkt,
    rx, rg, sx, sg, orx, org, osx, osg,
    wsend, wrecv, psend, precv, lsem,
    asend, arecv, bsend, brecv, csend, crecv, fsend, frecv,
    k1s, k1r, k2s, k2r, k3s, k3r,
):
    dp = lax.axis_index("dp")
    me = lax.axis_index("tm")
    z, c = dp // 2, dp % 2
    x, y = me // 4, me % 4
    partner = dp + 1 - 2 * c
    tms = [lax.rem(x + dx, 4) * 4 + lax.rem(y + dy, 4) for dx, dy in OFFS]
    zs = [lax.rem(z + k, 8) for k in range(8)]
    has13 = me % 5 == 0

    def remote(src, dst, ssem, rsem, **device):
        return pltpu.make_async_remote_copy(
            src_ref=src, dst_ref=dst, send_sem=ssem, recv_sem=rsem,
            device_id=device, device_id_type=MESH,
        )

    barrier = pltpu.get_barrier_semaphore()
    for t in tms:
        pl.semaphore_signal(barrier, inc=1, device_id={"tm": t}, device_id_type=MESH)
    for k in range(1, 8):
        pl.semaphore_signal(barrier, inc=1, device_id={"dp": zs[k] * 2 + c}, device_id_type=MESH)
    pl.semaphore_signal(barrier, inc=1, device_id={"dp": partner}, device_id_type=MESH)
    pl.semaphore_wait(barrier, 23)

    own = pltpu.make_async_copy(wl, wall.at[dp], lsem)
    own.start()
    for k in (4, 3, 5, 2, 6, 1, 7):
        remote(wl, wall.at[dp], wsend, wrecv.at[k], dp=zs[k] * 2 + c).start()
    remote(wl, wall.at[dp], psend, precv, dp=partner).start()

    def send_in(p, carry):
        for t in tms:
            remote(xt.at[p * 16 + t], xbuf.at[p, me], sx, rx.at[p], tm=t).start()
            remote(gt.at[p * 16 + t], gbuf.at[p, me], sg, rg.at[p], tm=t).start()
        pltpu.make_async_copy(xt.at[p * 16 + me], xbuf.at[p, me], rx.at[p]).start()
        pltpu.make_async_copy(gt.at[p * 16 + me], gbuf.at[p, me], rg.at[p]).start()
        return carry

    lax.fori_loop(0, 12, send_in, 0)
    for i in range(4):
        @pl.when(me != 5 * i)
        def _():
            remote(xt.at[192 + i], xbuf.at[12, me], sx, rx.at[12], tm=5 * i).start()
            remote(gt.at[192 + i], gbuf.at[12, me], sg, rg.at[12], tm=5 * i).start()

        @pl.when(me == 5 * i)
        def _():
            pltpu.make_async_copy(xt.at[192 + i], xbuf.at[12, me], rx.at[12]).start()
            pltpu.make_async_copy(gt.at[192 + i], gbuf.at[12, me], rg.at[12]).start()

    xbuf[13] = jnp.zeros_like(xbuf[13])
    gbuf[13] = jnp.zeros_like(gbuf[13])
    dw[...] = jnp.zeros_like(dw)
    gacc[...] = jnp.zeros_like(gacc)
    bacc[...] = jnp.zeros_like(bacc)

    for k in (1, 7, 2, 6, 3, 5, 4):
        source = lax.rem(z + 8 - k, 8) * 2 + c
        wait(wall.at[source], wrecv.at[k])
        remote(wall.at[source], wall.at[source], psend, precv, dp=partner).start()
    own.wait()
    wait(wall.at[pl.ds(0, 8)], precv)
    for d in range(16):
        wfull[48 * d : 48 * (d + 1), :] = wall[d, 0:48, :]
    gb[...] = jnp.sum(wall[:, 48:56, 0:D].astype(F32), axis=0)
    for j in range(9):
        wt[128 * j : 128 * (j + 1), :] = wfull[:, 128 * j : 128 * (j + 1)].T

    low = lax.broadcasted_iota(jnp.int32, (FR, 128), 1) < 64

    def group(s, carry):
        @pl.when(jnp.logical_or(s < 6, has13))
        def _():
            p0 = 2 * s
            wait(xbuf.at[p0], rx.at[p0])
            wait(gbuf.at[p0], rg.at[p0])

            @pl.when(s < 6)
            def _():
                wait(xbuf.at[p0 + 1], rx.at[p0 + 1])
                wait(gbuf.at[p0 + 1], rg.at[p0 + 1])

            def rows_of(i):
                return pl.ds(pl.multiple_of(i * 32, 32), 32)

            def tokens_of(i):
                return xbuf[p0 + i // 4, pl.ds((i % 4) * 4, 4)].astype(F32).reshape(32, D)

            def norm(i, carry):
                xx = tokens_of(i)
                m = jnp.mean(xx, axis=-1, keepdims=True)
                cc = xx - m
                r = lax.rsqrt(jnp.mean(cc * cc, axis=-1, keepdims=True) + EPS)
                normed[rows_of(i), :] = (cc * r * gb[0:1, :] + gb[1:2, :]).astype(BF)
                mst[rows_of(i), :] = jnp.broadcast_to(m, (32, 128))
                rst[rows_of(i), :] = jnp.broadcast_to(r, (32, 128))
                return carry

            lax.fori_loop(0, 8, norm, 0, unroll=2)

            for j in range(3):
                part = dot(normed[...], wfull[:, HD * j : HD * (j + 1)]).astype(BF)
                if j == 0:
                    part = part * jnp.asarray(0.125, BF)
                proj[:, HD * j : HD * (j + 1)] = part

            def attend(u, carry):
                rows = pl.ds(pl.multiple_of(u * FR, FR), FR)
                for h in range(3):
                    cols = slice(128 * h, 128 * (h + 1))
                    q = proj[rows, 128 * h : 128 * (h + 1)]
                    key = proj[rows, HD + 128 * h : HD + 128 * (h + 1)]
                    val = proj[rows, 2 * HD + 128 * h : 2 * HD + 128 * (h + 1)]
                    up = (gbuf[p0 + u, :, :, cols].astype(F32).reshape(FR, 128) * valid[...]).astype(BF)
                    none = jnp.zeros_like(key)
                    kk = jnp.concatenate([jnp.where(low, key, none), jnp.where(low, none, key)], axis=0)
                    vv = jnp.concatenate([jnp.where(low, val, none), jnp.where(low, none, val)], axis=0)
                    st = dot(kk, q, NT)
                    dpt = dot(vv, up, NT)
                    probs, grads = [], []
                    for half in range(2):
                        sc = st[FR * half : FR * (half + 1)] + mask[...]
                        e = jnp.exp(sc - jnp.max(sc, axis=0, keepdims=True))
                        pr = e * (1.0 / jnp.sum(e, axis=0, keepdims=True))
                        dd = dpt[FR * half : FR * (half + 1)]
                        inner = jnp.sum(pr * dd, axis=0, keepdims=True)
                        probs.append(pr.astype(BF))
                        grads.append((pr * (dd - inner)).astype(BF))
                    pb = jnp.concatenate(probs, axis=0)
                    ds = jnp.concatenate(grads, axis=0)
                    mixed = dot(pb, vv, TN) * valid[...]
                    abuf[p0 + u, :, :, cols] = mixed.reshape(16, 8, 128).astype(BF)
                    dq = dot(ds, kk, TN) * 0.125
                    dvf = dot(pb, up)
                    dkf = dot(ds, q)
                    dproj[rows, 128 * h : 128 * (h + 1)] = dq.astype(BF)
                    dproj[rows, HD + 128 * h : HD + 128 * (h + 1)] = jnp.where(low, dkf[:FR], dkf[FR:]).astype(BF)
                    dproj[rows, 2 * HD + 128 * h : 2 * HD + 128 * (h + 1)] = jnp.where(low, dvf[:FR], dvf[FR:]).astype(BF)
                return carry

            lax.fori_loop(0, 2, attend, 0)

            for j in range(3):
                ng[:, 256 * j : 256 * (j + 1)] = dot(dproj[...], wt[:, 256 * j : 256 * (j + 1)]).astype(BF)

            def back(i, carry):
                std = (tokens_of(i) - mst[rows_of(i), 0:1]) * rst[rows_of(i), 0:1]
                n = ng[rows_of(i), :].astype(F32)
                gacc[...] += jnp.sum((n * std).reshape(4, 8, D), axis=0)
                bacc[...] += jnp.sum(n.reshape(4, 8, D), axis=0)
                e = n * gb[0:1, :]
                m1 = jnp.mean(e, axis=-1, keepdims=True)
                m2 = jnp.mean(e * std, axis=-1, keepdims=True)
                tg = rst[rows_of(i), 0:1] * (e - m1 - std * m2)
                tbuf[p0 + i // 4, pl.ds((i % 4) * 4, 4)] = tg.reshape(4, 8, D).astype(BF)
                return carry

            lax.fori_loop(0, 8, back, 0, unroll=2)

            for u in range(2):
                p = p0 + u

                @pl.when(p < 13)
                def _():
                    last = p // 12
                    patch = jnp.where(p < 12, 16 * p + me, 192 + me // 5)
                    for t in tms:
                        remote(tbuf.at[p, t], tgo.at[patch], osx.at[last], orx.at[last], tm=t).start()
                        remote(abuf.at[p, t], ato.at[patch], osg.at[last], org.at[last], tm=t).start()
                    pltpu.make_async_copy(tbuf.at[p, me], tgo.at[patch], orx.at[last]).start()
                    pltpu.make_async_copy(abuf.at[p, me], ato.at[patch], org.at[last]).start()

            nt[...] = normed[...].T
            for j in range(3):
                dw[:, HD * j : HD * (j + 1)] += dot(nt[...], dproj[:, HD * j : HD * (j + 1)])

        return carry

    lax.fori_loop(0, 7, group, 0)

    def block(d):
        return dw[pl.ds(pl.multiple_of(d * 48, 8), 48), :]

    order = (4, 3, 5, 2, 6, 1, 7, 0)
    gsum = jnp.sum(gacc[...], axis=0, keepdims=True)
    bsum = jnp.sum(bacc[...], axis=0, keepdims=True)
    pk[...] = jnp.zeros_like(pk)
    for j in range(3):
        pk[j : j + 1, :] = gsum[:, 256 * j : 256 * (j + 1)]
        pk[3 + j : 4 + j, :] = bsum[:, 256 * j : 256 * (j + 1)]
    for k in order:
        senda[k] = block(zs[k] * 2 + 1 - c).astype(BF)
        remote(senda.at[k], recva.at[k], asend, arecv.at[k], dp=partner).start()
    remote(pk, pkp, k1s, k1r, dp=partner).start()
    for k in order:
        wait(recva.at[k], arecv.at[k])
        total = block(zs[k] * 2 + c) + recva[k].astype(F32)
        if k:
            sendb[k - 1] = total.astype(BF)
            remote(sendb.at[k - 1], recvb.at[k - 1], bsend, brecv.at[k - 1], dp=zs[k] * 2 + c).start()
    wait(pkp, k1r)
    pk2[...] = pk[...] + pkp[...]
    for k in range(1, 8):
        remote(pk2, pkz.at[k - 1], k2s, k2r.at[k - 1], dp=zs[k] * 2 + c).start()
    for k in (1, 7, 2, 6, 3, 5, 4):
        wait(recvb.at[k - 1], brecv.at[k - 1])
        total = total + recvb[k - 1].astype(F32)
    for j in range(9):
        totb[j] = total[:, 128 * j : 128 * (j + 1)].astype(BF)

        @pl.when(me != j)
        def _():
            remote(totb.at[j], crx.at[me], csend, crecv, tm=j).start()

        @pl.when(me == j)
        def _():
            pltpu.make_async_copy(totb.at[j], crx.at[me], crecv).start()

    packed = pk2[...]
    for k in range(1, 8):
        wait(pkz.at[k - 1], k2r.at[k - 1])
        packed = packed + pkz[k - 1]
    pk3[...] = packed
    for t in tms:
        remote(pk3, pkt.at[me], k3s, k3r, tm=t).start()
    pltpu.make_async_copy(pk3, pkt.at[me], k3r).start()

    @pl.when(me < 9)
    def _():
        wait(crx, crecv)
        red[...] = jnp.sum(crx[...].astype(F32), axis=0).astype(BF)
        for t in tms:
            remote(red, fin.at[me], fsend, frecv, tm=t).start()
        pltpu.make_async_copy(red, fin.at[me], frecv).start()

    wait(pkt, k3r)
    gbo[...] = jnp.sum(pkt[...], axis=0)
    wait(fin, frecv)
    for j in range(9):
        dwo[:, 128 * j : 128 * (j + 1)] = fin[j].astype(F32)

    wait(tgo.at[pl.ds(0, 192)], orx.at[0])
    wait(ato.at[pl.ds(0, 192)], org.at[0])
    wait(tgo.at[pl.ds(192, 4)], orx.at[1])
    wait(ato.at[pl.ds(192, 4)], org.at[1])
    wait(tgo.at[pl.ds(0, 180)], osx.at[0])
    wait(ato.at[pl.ds(0, 180)], osg.at[0])

    @pl.when(has13)
    def _():
        wait(tgo.at[pl.ds(0, 15)], osx.at[1])
        wait(ato.at[pl.ds(0, 15)], osg.at[1])
        wait(xt.at[pl.ds(0, 183)], sx)
        wait(gt.at[pl.ds(0, 183)], sg)

    @pl.when(jnp.logical_not(has13))
    def _():
        wait(xt.at[pl.ds(0, 184)], sx)
        wait(gt.at[pl.ds(0, 184)], sg)

    wait(wall.at[pl.ds(0, 7)], wsend)
    wait(wall.at[pl.ds(0, 8)], psend)
    wait(senda, asend)
    wait(sendb, bsend)
    wait(pk, k1s)
    wait(pkz, k2s)
    wait(pkt.at[pl.ds(0, 15)], k3s)

    @pl.when(me < 9)
    def _():
        wait(totb.at[pl.ds(0, 8)], csend)
        wait(crx.at[pl.ds(0, 15)], fsend)

    @pl.when(me >= 9)
    def _():
        wait(totb, csend)


def masks(frame_count, starts, kept):
    index = jnp.arange(FR, dtype=jnp.int32)
    clip = jnp.zeros((FR,), jnp.int32)
    for b in range(1, starts.shape[0]):
        clip = clip + jnp.where(index >= b * BLOCK, starts[b], 0)
    usable = (index < frame_count) & (kept == 1)
    allowed = (clip[:, None] == clip[None, :]) & (usable[:, None] | (index[:, None] == index[None, :]))
    valid = jnp.broadcast_to((index < frame_count)[:, None], (FR, 128))
    return jnp.where(allowed, 0.0, MASKED).astype(F32), jnp.where(valid, 1.0, 0.0).astype(F32)


def body(video_tokens, norm_gain, norm_bias, qkv_weight, frame_counts, clip_starts, frame_kept, attended_grad):
    dp = lax.axis_index("dp")
    xt = video_tokens[0].transpose(1, 0, 2)
    gt = attended_grad[0].transpose(1, 0, 2)
    mask, valid = masks(frame_counts[0], clip_starts[0], frame_kept[0])
    rows = jnp.zeros((8, C), BF)
    rows = lax.dynamic_update_slice(rows, jnp.stack([norm_gain, norm_bias]), (0, dp * 48))
    wl = jnp.concatenate([qkv_weight, rows], axis=0)
    vmem = pltpu.VMEM
    sems = pltpu.SemaphoreType.DMA
    any_spec = pl.BlockSpec(memory_space=pl.ANY)
    vspec = pl.BlockSpec(memory_space=pltpu.VMEM)
    ato, tgo, dwo, gbo = pl.pallas_call(
        kernel,
        out_shape=(
            jax.ShapeDtypeStruct((196, 8, HD), BF),
            jax.ShapeDtypeStruct((196, 8, D), BF),
            jax.ShapeDtypeStruct((48, C), F32),
            jax.ShapeDtypeStruct((8, 256), F32),
        ),
        in_specs=[any_spec, any_spec, any_spec, vspec, vspec],
        out_specs=(any_spec, any_spec, vspec, vspec),
        scratch_shapes=[
            vmem((14, 16, 8, D), BF), vmem((14, 16, 8, HD), BF),
            vmem((14, 16, 8, HD), BF), vmem((14, 16, 8, D), BF),
            vmem((16, WB, C), BF), vmem((D, C), BF), vmem((C, D), BF), vmem((D, C), F32), vmem((8, D), F32),
            vmem((256, D), BF), vmem((256, 128), F32), vmem((256, 128), F32),
            vmem((256, C), BF), vmem((256, C), BF), vmem((D, 256), BF), vmem((256, D), BF),
            vmem((8, D), F32), vmem((8, D), F32),
            vmem((8, 48, C), BF), vmem((8, 48, C), BF), vmem((7, 48, C), BF), vmem((7, 48, C), BF),
            vmem((9, 48, 128), BF), vmem((16, 48, 128), BF), vmem((48, 128), BF), vmem((9, 48, 128), BF),
            vmem((8, 256), F32), vmem((8, 256), F32), vmem((8, 256), F32), vmem((7, 8, 256), F32),
            vmem((8, 256), F32), vmem((16, 8, 256), F32),
            sems((13,)), sems((13,)), sems, sems, sems((2,)), sems((2,)), sems((2,)), sems((2,)),
            sems, sems((8,)), sems, sems, sems,
            sems, sems((8,)), sems, sems((7,)), sems, sems, sems, sems,
            sems, sems, sems, sems((7,)), sems, sems,
        ],
        compiler_params=pltpu.CompilerParams(
            collective_id=0, has_side_effects=True, vmem_limit_bytes=58 * 2**20
        ),
    )(xt, gt, wl, mask, valid)
    attended = ato.transpose(1, 0, 2)[None]
    tokens_grad = tgo.transpose(1, 0, 2)[None]
    flat = gbo.reshape(2048)
    gain = lax.dynamic_slice(flat, (dp * 48,), (48,))
    bias = lax.dynamic_slice(flat, (D + dp * 48,), (48,))
    return attended, tokens_grad, dwo, gain, bias


def solution(mesh):
    placed = (
        P("dp", "tm", None, None), P("dp"), P("dp"), P("dp", None),
        P("dp"), P("dp", None), P("dp", None), P("dp", "tm", None, None),
    )
    return jax.shard_map(
        body,
        mesh=mesh,
        in_specs=placed,
        out_specs=(P("dp", "tm", None, None), P("dp", "tm", None, None), P("dp", None), P("dp"), P("dp")),
        check_vma=False,
    )
```

time: 467 us -> 140 us (0.30)
  waiting for transfers between devices: 142 us -> 0 us
  Pallas kernels: 0 us -> 122 us
  blocking collectives: 118 us -> 0 us
  local copies, waits for them, and re-layouts: 76.8 us -> 8.51 us
  matrix products: 61.1 us -> 0 us
  starting transfers between devices: 27.5 us -> 0 us
  between operations: 15.9 us -> 1.32 us
  other arithmetic: 22.6 us -> 8.06 us
    pallas_call x0 -> x1, Pallas kernels: none -> 122 us  [body(): pl.pallas_call(kernel, out_shape=(jax.ShapeDtypeStruct((196, 8, HD), BF),...]
    all_to_all x4 -> x0, waiting for transfers between devices: 98.4 us -> none  [the longest x2 69.6 us: to_frames(): lax.all_to_all(patch_rows, 'tm', split_axis=0, concat_axis=1, tiled=True)]
    unnamed x2 -> x0, blocking collectives: 82.9 us -> none
    dot_general x8 -> x0, matrix products: 55.3 us -> none  [the longest x1 10.1 us: attend_back(): jnp.einsum('phfg,fphd->gphd', score_grad, queries, preferred_element_type...]
    psum x1 -> x0, waiting for transfers between devices: 43.1 us -> none  [body(): lax.psum(shares[0].astype(jnp.bfloat16), 'tm').astype(jnp.float32)]
    psum x1 -> x0, blocking collectives: 34.8 us -> none  [body(): lax.psum(shares[1].astype(jnp.bfloat16), 'tm').astype(jnp.float32)]
    all_to_all x4 -> x0, starting transfers between devices: 26.9 us -> none  [the longest x2 14.2 us: to_patches(): lax.all_to_all(widened, 'tm', split_axis=1, concat_axis=0, tiled=True)]
    reshape x7 -> x0, local copies, waits for them, and re-layouts: 22 us -> none  [the longest x3 8.89 us: attend_back(): piece.reshape(frames, patch_rows, joined)]
  transfers between devices with their start and end apart: 7 -> 0, of which waited for: 4 -> 0; matrix products, arithmetic and copies ran while one was open for 16% -> 0% of each run, Pallas kernels for 0% -> 0%
where the time goes in v1:
time: 140 us
  Pallas kernels  122 us (87%)
  local copies, waits for them, and re-layouts  8.51 us (6%)
  other arithmetic  8.06 us (6%)
    pallas_call x1, Pallas kernels, body(): pl.pallas_call(kernel, out_shape=(jax.ShapeDtypeStruct((196, 8, HD), BF),...  122 us
    unnamed x8, local copies, waits for them, and re-layouts  5.39 us
    add x1, other arithmetic, masks(): clip = clip + jnp.where(index >= b * BLOCK, starts[b], 0)  4.42 us

profile of v1, /device:TPU:24, one launch (start us, length us, event | category | flops | bytes accessed | tf_op | source)
XLA Modules:
  0.0 139.9 jit_solution(17199344658383090720)
XLA Ops:
  0.6 1.5 %fusion.10 = (s32[1,1]{1,0:T(1,128)}, s32[1,1]{1,0:T(1,128)}, s32[1,1]{1,0:T(1,128)}, s32[1,1]{1,0:T(1,128)}, s32[1,1]{1,0:T(1,128)}, /*index=5*/s32[1,1]{1,0:T(1,128)}, s32[1,1]{1,0:T(1,128)}) fusion(s32[1,8]{1,0:T(1,128)} %param.13), kind=kLoop, calls=%fused_computation.22 | loop fusion | bytes 56 | tf_op jit(solution)/shard_map/slice | solution.py:328
  2.1 4.4 %fusion.8 = s32[128]{0:T(128)S(1)} fusion(s32[]{:T(128)} %bitcast.12, s32[]{:T(128)} %bitcast.11, s32[]{:T(128)} %bitcast.10, s32[]{:T(128)} %bitcast.9, s32[]{:T(128)} %bitcast.8, s32[]{:T(128)} %bitcast.7, s32[]{:T(128)} %bitcast.6), kind=kLoop, calls=%fused_computation.19 | loop fusion | flops 2560 | bytes 540 | tf_op jit(solution)/shard_map/add | solution.py:328
  7.2 0.7 bitcast_and_fusion
  7.9 0.7 fusion.2.mask
  8.6 0.7 pad_maximum_fusion.1
  9.3 0.3 dynamic_update_slice.3
  9.6 1.6 %pad_maximum_fusion.wl = bf16[56,1152]{1,0:T(8,128)(2,1)} fusion(bf16[8,1152]{1,0:T(8,128)(2,1)S(1)} %dynamic_update_slice.3, bf16[48,1152]{1,0:T(8,128)(2,1)} %param.11), kind=kLoop, calls=%fused_computation | loop fusion | flops 258048 | bytes 258048 | tf_op jit(solution)/shard_map/concatenate | solution.py:342
  11.2 0.7 broadcast_in_dim.79.valid
  11.9 122.0 %shard_map.119 = (bf16[196,8,384]{2,1,0:T(8,128)(2,1)}, bf16[196,8,768]{2,1,0:T(8,128)(2,1)}, f32[48,1152]{1,0:T(8,128)}, f32[8,256]{1,0:T(8,128)}) custom-call(bf16[196,8,768]{2,1,0:T(8,128)(2,1)} %bitcast.28, bf16[196,8,384]{2,1,0:T(8,128)(2,1)} %bitcast.31, bf16[56,1152]{1,0:T(8,128)(2,1)} %pad_maximum_fusion.wl, f32[128,128]{1,0:T(8,128)} %fusion.2.mask, ...), custom_call_target="tpu_custom_call" | custom-call | tf_op jit(solution)/shard_map/pallas_call | solution.py:347
  133.9 0.0 copy-start
  133.9 0.9 copy.13
  134.7 0.6 fusion.9
  135.3 2.4 %copy.19 = bf16[1,8,196,384]{3,1,2,0:T(8,128)(2,1)} copy(bf16[1,8,196,384]{3,1,2,0:T(8,128)(2,1)} %bitcast.30) | data formatting | bytes 2408448
  137.7 0.0 copy-done
  137.7 0.0 copy-start.1
  137.8 1.4 %copy.20 = bf16[1,8,196,768]{3,1,2,0:T(8,128)(2,1)} copy(bf16[1,8,196,768]{3,1,2,0:T(8,128)(2,1)S(1)} %bitcast.29) | data formatting | bytes 4816896
  139.2 0.0 copy-done.1
  139.2 0.7 copy.21
  (2 shorter events, 0.0 us)
Async XLA Ops:
  133.9 3.9 %copy-start = (bf16[196,8,768]{2,1,0:T(8,128)(2,1)S(1)}, bf16[196,8,768]{2,1,0:T(8,128)(2,1)}, u32[]{:S(2)}) copy-start(bf16[196,8,768]{2,1,0:T(8,128)(2,1)} %get-tuple-element.10) | copy-start | bytes 7225348
  137.7 1.4 %copy-start.1 = (f32[48,1152]{1,0:T(8,128)S(1)}, f32[48,1152]{1,0:T(8,128)}, u32[]{:S(2)}) copy-start(f32[48,1152]{1,0:T(8,128)} %get-tuple-element.29) | copy-start | bytes 663556
